TPU v7x, 128 devices: a whole 4x4x4 slice. The times are simulated.
128 devices in a mesh: row: 8 (over x_lo, z), col: 16 (over x_hi, y, core).
Axes of the slice: x: 4 (x_hi: 2, x_lo: 2; x = x_hi * 2 + x_lo), y: 4, z: 4, core: 2. Of those that a mesh axis runs over, the one named last changes fastest.
Arguments:
- ancestor: float32 [24576, 24576], P('row', 'col'), may hold values from -6 to 6
- lhat_one: float32 [24576, 512], P('col', 'row'), may hold values from -0.15625 to 0.15625
- lhat_two: float32 [24576, 512], P('col', 'row'), may hold values from -0.15625 to 0.15625
- link_two: float32 [512, 512], replicated, may hold values from -0.25 to 0.25
- diag_one: float32 [512, 512], replicated, may hold values from -6 to 6
- diag_two: float32 [512, 512], replicated, may hold values from -6 to 6
- mask_one: int32 [192], replicated, may hold values from 0 to 1, as said below
- mask_two: int32 [192], replicated, may hold values from 0 to 1, as said below
Outputs:
- x_one: float32 [24576, 512], P('row', 'col')
- d_one: float32 [512, 512], replicated
- x_two: float32 [24576, 512], P('row', 'col')
- link_inverse: float32 [512, 512], replicated
- d_two: float32 [512, 512], replicated
Inputs may be any that keep to these rules, and one draw needn't show every extreme that they name: `mask_one`: 1 where a block of 128 factor rows is nonzero, else 0; the last block is always nonzero. `mask_two`: 1 where a block of 128 factor rows is nonzero, else 0; the last block is always nonzero.
All inputs are finite; a program needn't handle non-finite values.
Results may differ from a plain program's by a relative error of at most 0.00011.
Values sent between devices are 32-bit elements; how exact they have to be, the bound alone decides.
No kernel may reach another device: no remote copies, remote signals or barrier semaphores. Data moves between devices by JAX's collectives and lax.ppermute only.
A program may use at most 128 MiB of HBM per device.

v0:
```python
import jax
import jax.numpy as jnp
from jax import lax
from jax.sharding import Mesh, PartitionSpec as P

BLOCK = 128
ROW = ("xl", "z")
COL = ("xh", "y", "core")
ALL = ROW + COL
SIZES = (2, 4, 2, 4, 2)
SWAP = ((0, 1), (1, 0))


def product(left, right, contract=((1,), (0,))):
    return lax.dot_general(
        left,
        right,
        (contract, ((), ())),
        precision=lax.Precision.HIGH,
        preferred_element_type=jnp.float32,
    )


def linear(xl, z, xh, y, core):
    return (((xl * 4 + z) * 2 + xh) * 4 + y) * 2 + core


def factor_routes():
    routes = []
    for xl in range(2):
        for z in range(4):
            for xh in range(2):
                for y in range(4):
                    for core in range(2):
                        source = linear(y // 2, y % 2 * 2 + core, xl, z, xh)
                        routes.append((source, linear(xl, z, xh, y, core)))
    return routes


def per_device(ancestor, lhat_one, lhat_two, link_two, diag_one, diag_two, mask_one, mask_two):
    row_index = lax.axis_index(ROW)
    column_index = lax.axis_index(COL)
    core = lax.axis_index("core")
    xh = lax.axis_index("xh")
    rows, depth = ancestor.shape
    width = link_two.shape[0]
    blocks = depth // BLOCK
    part = rows // 16

    def masked(shard, mask):
        own = lax.dynamic_slice_in_dim(mask, column_index * blocks, blocks).astype(jnp.float32)
        return (shard.reshape(blocks, BLOCK, -1) * own[:, None, None]).reshape(shard.shape)

    def row_sum(factor):
        partial = product(ancestor, factor).reshape(2, 4, 2, part, width)
        keep = lax.dynamic_index_in_dim(partial, core, 2, keepdims=False)
        send = lax.dynamic_index_in_dim(partial, 1 - core, 2, keepdims=False)
        chip = keep + lax.ppermute(send, "core", SWAP)
        chip = chip.transpose(1, 0, 2, 3).reshape(8 * part, width)
        line = lax.psum_scatter(chip, "y", scatter_dimension=0, tiled=True).reshape(2, part, width)
        own = lax.dynamic_index_in_dim(line, xh, 0, keepdims=False)
        other = lax.dynamic_index_in_dim(line, 1 - xh, 0, keepdims=False)
        return own + lax.ppermute(other, "xh", SWAP)

    factor_one = lax.all_gather(masked(lhat_one, mask_one), ROW, axis=1, tiled=True)
    factor_two = lax.all_gather(masked(lhat_two, mask_two), ROW, axis=1, tiled=True)
    local = jnp.concatenate(
        [lax.dynamic_slice_in_dim(f, row_index * part, part, 0) for f in (factor_one, factor_two)],
        axis=1,
    )
    local = lax.ppermute(local, ALL, factor_routes())
    sum_one = row_sum(factor_one)
    sum_two = row_sum(factor_two)
    gram_one = product(local, sum_one, ((0,), (0,)))
    gram_two = product(local[:, width:], sum_two, ((0,), (0,)))
    grams = jnp.concatenate([gram_one, gram_two], axis=0)
    half = grams.shape[0] // 2
    keep = lax.dynamic_slice_in_dim(grams, core * half, half, 0)
    send = lax.dynamic_slice_in_dim(grams, (1 - core) * half, half, 0)
    piece = keep + lax.ppermute(send, "core", SWAP)
    piece = lax.psum_scatter(piece, "y", scatter_dimension=0, tiled=True)
    piece = lax.psum_scatter(piece, "z", scatter_dimension=0, tiled=True)
    piece = lax.psum(piece, ("xl", "xh"))
    piece = lax.all_gather(piece, "z", axis=0, tiled=True)
    piece = lax.all_gather(piece, "y", axis=0, tiled=True)
    other = lax.ppermute(piece, "core", SWAP)
    grams = jnp.where(
        core == 0, jnp.concatenate([piece, other], 0), jnp.concatenate([other, piece], 0)
    )
    cross = grams[width : 2 * width]
    d_one = diag_one + grams[:width]
    link_inverse = cross.T - product(d_one, link_two)
    d_two = (
        diag_two
        + grams[2 * width :]
        - product(cross, link_two)
        - product(link_two, link_inverse, ((0,), (0,)))
    )
    own_two = product(sum_one, link_two) - sum_two
    out = jnp.stack([-sum_one, own_two], axis=0)
    out = lax.all_to_all(out, COL, split_axis=2, concat_axis=1, tiled=True)
    return (out[0], d_one, out[1], link_inverse, d_two)


def solution(mesh):
    fine = Mesh(mesh.devices.reshape(SIZES), ALL)
    in_specs = (P(ROW, COL), P(COL, ROW), P(COL, ROW), P(), P(), P(), P(), P())
    out_specs = (P(ROW, COL), P(), P(ROW, COL), P(), P())
    return jax.shard_map(
        per_device, mesh=fine, in_specs=in_specs, out_specs=out_specs, check_vma=False
    )
```

profile of v0, /device:TPU:1, one launch (start us, length us, event | category | flops | bytes accessed | tf_op | source)
XLA Modules:
  0.0 407.2 jit_solution(15928660699130049153)
XLA Ops:
  7.2 0.8 dynamic-slice_convert_fusion
  8.1 0.1 broadcast_bitcast_fusion.1
  8.2 1.8 broadcast_multiply_fusion.1
  10.0 0.0 all-gather.6.cloned.1.call-start
  10.0 0.1 broadcast_bitcast_fusion
  10.1 1.8 broadcast_multiply_fusion
  11.9 43.3 %all-gather.4.cloned.1.call-done = f32[1536,512]{0,1:T(8,128)} async-done(((f32[1536,64]{0,1:T(8,128)}), f32[1536,512]{0,1:T(8,128)}) %all-gather.4.cloned.1.call-update) | async-done | bytes 3145744 | tf_op jit(solution)/shard_map/all_gather | solution.py:65
  55.2 20.6 %convolution_bitcast_fusion.1 = f32[3072,512]{0,1:T(8,128)} fusion(f32[1536,512]{0,1:T(8,128)} %all-gather.4.cloned.1.call-done, f32[3072,1536]{1,0:T(8,128)} %param.8), kind=kOutput, calls=%fused_computation.1 | convolution fusion | flops 14495514624 | bytes 28311552 | tf_op jit(solution)/shard_map/dot_general | solution.py:15
  75.8 6.6 %copy.48 = f32[3072,512]{1,0:T(8,128)} copy(f32[3072,512]{0,1:T(8,128)} %convolution_bitcast_fusion.1) | data formatting | bytes 12582912 | tf_op jit(solution)/shard_map/dot_general | solution.py:15
  82.5 3.9 dynamic-slice_bitcast_fusion.1
  86.4 3.0 collective-permute-start
  89.4 5.6 %collective-permute-done = f32[2,4,192,512]{3,2,1,0:T(8,128)} collective-permute-done((f32[2,4,192,512]{3,2,1,0:T(8,128)}, f32[2,4,192,512]{3,2,1,0:T(8,128)}, u32[]{:S(2)}, u32[]{:S(2)}) %collective-permute-start) | collective-permute-done | bytes 3145760 | tf_op jit(solution)/shard_map/ppermute | solution.py:58
  95.1 3.6 fusion.1
  98.7 2.0 copy.49
  100.8 0.0 reduce-scatter.7.cloned.1.call-start
  100.8 0.5 all-gather.6.cloned.1.call-done
  101.3 20.6 %convolution_bitcast_fusion = f32[3072,512]{0,1:T(8,128)} fusion(f32[1536,512]{0,1:T(8,128)} %all-gather.6.cloned.1.call-done, f32[3072,1536]{1,0:T(8,128)} %param.8), kind=kOutput, calls=%fused_computation | convolution fusion | flops 14495514624 | bytes 28311552 | tf_op jit(solution)/shard_map/dot_general | solution.py:15
  121.9 6.6 %copy.50 = f32[3072,512]{1,0:T(8,128)} copy(f32[3072,512]{0,1:T(8,128)} %convolution_bitcast_fusion) | data formatting | bytes 12582912 | tf_op jit(solution)/shard_map/dot_general | solution.py:15
  128.5 2.4 dynamic-slice_bitcast_fusion
  130.9 3.3 collective-permute-start.2
  134.2 5.3 %collective-permute-done.2 = f32[2,4,192,512]{3,2,1,0:T(8,128)S(1)} collective-permute-done((f32[2,4,192,512]{3,2,1,0:T(8,128)S(1)}, f32[2,4,192,512]{3,2,1,0:T(8,128)S(1)}, u32[]{:S(2)}, u32[]{:S(2)}) %collective-permute-start.2) | collective-permute-done | bytes 3145760 | tf_op jit(solution)/shard_map/ppermute | solution.py:58
  139.5 0.7 fusion
  140.3 1.9 copy.51
  142.3 1.3 constant_dynamic-slice_fusion
  143.6 1.4 constant_dynamic-slice_fusion.1
  145.0 0.1 pad_maximum_fusion
  145.1 0.3 copy.55
  145.4 4.6 %collective-permute-start.4 = (f32[192,1024]{1,0:T(8,128)S(1)}, f32[192,1024]{1,0:T(8,128)S(1)}, u32[]{:S(2)}, u32[]{:S(2)}) collective-permute-start(f32[192,1024]{1,0:T(8,128)S(1)} %copy.55), channel_id=1, source_target_pairs={{0,0},{16,1},{32,2},{48,3},{64,4},{80,5},{96,6},{112,7},{1,8},{17,... | collective-permute-start | bytes 2359304 | tf_op jit(solution)/shard_map/ppermute | solution.py:71
  150.1 1.0 dynamic-slice_bitcast_fusion.3
  151.1 0.6 collective-permute-start.1
  151.7 44.6 %reduce-scatter.7.cloned.1.call-done = f32[384,512]{1,0:T(8,128)} async-done(((f32[1536,512]{1,0:T(8,128)}), f32[384,512]{1,0:T(8,128)}) %reduce-scatter.7.cloned.1.call-update) | async-done | bytes 786448 | tf_op jit(solution)/shard_map/reduce_scatter | solution.py:60
  196.3 1.8 dynamic-slice_bitcast_fusion.2
  198.1 4.6 %collective-permute-start.3 = (f32[192,512]{1,0:T(8,128)}, f32[192,512]{1,0:T(8,128)S(1)}, u32[]{:S(2)}, u32[]{:S(2)}) collective-permute-start(f32[192,512]{1,0:T(8,128)} %dynamic-slice_bitcast_fusion.2), channel_id=1, source_target_pairs={{0,8},{8,0},{1,9},{9,1},{2,10},{10,2},{3,11},{11,3},{4,12},{12,4},... | collective-permute-start | bytes 1179656 | tf_op jit(solution)/shard_map/ppermute | solution.py:63
  202.7 1.9 negate_bitcast_fusion
  204.6 7.3 %collective-permute-done.3 = f32[192,512]{1,0:T(8,128)S(1)} collective-permute-done((f32[192,512]{1,0:T(8,128)}, f32[192,512]{1,0:T(8,128)S(1)}, u32[]{:S(2)}, u32[]{:S(2)}) %collective-permute-start.3) | collective-permute-done | bytes 393248 | tf_op jit(solution)/shard_map/ppermute | solution.py:63
  212.0 1.8 fusion.10
  213.8 2.6 fusion.14
  216.4 1.7 fusion.2
  218.1 1.0 collective-permute-start.5
  219.1 3.4 collective-permute-done.5
  222.5 3.4 fusion.4
  226.0 25.9 %reduce-scatter.9.cloned.1.call-done = f32[192,512]{1,0:T(8,128)} async-done(((f32[768,512]{1,0:T(8,128)}), f32[192,512]{1,0:T(8,128)}) %reduce-scatter.9.cloned.1.call-update) | async-done | bytes 393232 | tf_op jit(solution)/shard_map/reduce_scatter | solution.py:81
  252.0 21.9 %reduce-scatter.11.cloned.1.call-done = f32[48,512]{1,0:T(8,128)} async-done(((f32[192,512]{1,0:T(8,128)}), f32[48,512]{1,0:T(8,128)}) %reduce-scatter.11.cloned.1.call-update) | async-done | bytes 98320 | tf_op jit(solution)/shard_map/reduce_scatter | solution.py:82
  273.9 43.5 %all-reduce.2.cloned.1.call-done = f32[48,512]{1,0:T(8,128)} async-done(((f32[48,512]{1,0:T(8,128)}), f32[48,512]{1,0:T(8,128)}) %all-reduce.2.cloned.1.call-update) | async-done | bytes 98320 | tf_op jit(solution)/shard_map/psum | solution.py:83
  317.4 12.7 %all_gather.14 = f32[192,512]{1,0:T(8,128)} all-gather(f32[48,512]{1,0:T(8,128)} %all-reduce.2.cloned.1.call-done), channel_id=1, replica_groups=mesh['xl'=2,'z'=4,'xh'=2,'y'=4,'core'=2] {'z'}, dimensions={0}, use_global_device_ids=true | all-gather | bytes 491520 | tf_op jit(solution)/shard_map/all_gather | solution.py:84
  330.1 30.0 %all-gather.8.cloned.1.call-done = f32[768,512]{1,0:T(8,128)} async-done(((f32[192,512]{1,0:T(8,128)}), f32[768,512]{1,0:T(8,128)}) %all-gather.8.cloned.1.call-update) | async-done | bytes 1572880 | tf_op jit(solution)/shard_map/all_gather | solution.py:85
  360.1 0.8 collective-permute-start.6
  360.9 0.5 fusion.5
  361.4 0.1 pad_maximum_fusion.1
  361.5 1.3 copy.52
  362.8 5.5 %all-to-all-start = ((f32[2,192,512]{1,0,2:T(2,128)}), f32[2,192,512]{1,0,2:T(2,128)S(1)}, u32[]{:S(2)}, u32[]{:S(2)}) async-start(f32[2,192,512]{1,0,2:T(2,128)} %copy.52), calls=%async_computation.2 | async-start | bytes 2097152 | tf_op jit(solution)/shard_map/all_to_all | solution.py:101
  368.3 17.1 %all-to-all-done = f32[2,192,512]{1,0,2:T(2,128)S(1)} async-done(((f32[2,192,512]{1,0,2:T(2,128)}), f32[2,192,512]{1,0,2:T(2,128)S(1)}, u32[]{:S(2)}, u32[]{:S(2)}) %all-to-all-start) | async-done | bytes 786464 | tf_op jit(solution)/shard_map/all_to_all | solution.py:101
  385.4 0.1 copy.53
  385.5 0.1 fusion.13
  385.6 0.3 copy.54
  385.9 1.0 squeeze.40
  386.9 0.3 copy.56
  387.2 1.0 squeeze.41
  388.1 3.7 maximum_select_fusion
  391.8 2.0 fusion.8
  393.8 0.2 slice_add_fusion.1
  394.0 1.1 bitcast_subtract_fusion
  395.1 1.3 copy.59
  396.4 3.9 fusion.7
  (40 shorter events, 0.5 us)
Async XLA Ops:
  7.2 353.7 %copy-start = (f32[512,512]{1,0:T(8,128)S(1)}, f32[512,512]{1,0:T(8,128)}, u32[]{:S(2)}) copy-start(f32[512,512]{1,0:T(8,128)} %param.11) | copy-start | bytes 3145732
  7.2 48.0 %all-gather.4.cloned.1.call-start = ((), (), s32[]{:S(2)}) async-start(), calls=%async_computation.5 | async-start | bytes 3538944 | tf_op jit(solution)/shard_map/all_gather | solution.py:65
  10.0 91.3 %all-gather.6.cloned.1.call-start = ((), (), s32[]{:S(2)}) async-start(), calls=%async_computation.7 | async-start | bytes 3538944 | tf_op jit(solution)/shard_map/all_gather | solution.py:66
  11.9 138.2 %reduce-scatter.5.cloned.1.call-start = ((), (), s32[]{:S(2)}) async-start(), calls=%async_computation.6 | async-start | bytes 3932160 | tf_op jit(solution)/shard_map/reduce_scatter | solution.py:60
  86.4 8.7 %collective-permute-start = (f32[2,4,192,512]{3,2,1,0:T(8,128)}, f32[2,4,192,512]{3,2,1,0:T(8,128)}, u32[]{:S(2)}, u32[]{:S(2)}) collective-permute-start(f32[2,4,192,512]{3,2,1,0:T(8,128)} %dynamic-slice_bitcast_fusion.1), channel_id=1, source_target_pairs={{0,1},{1,0},{2,3},{3,2},{4,5},{5,4},{6,7},{7,6},{8,9},{9,8},{10,11... | collective-permute-start | bytes 9437192 | tf_op jit(solution)/shard_map/ppermute | solution.py:58
  100.8 95.5 %reduce-scatter.7.cloned.1.call-start = ((), (), s32[]{:S(2)}) async-start(), calls=%async_computation.8 | async-start | bytes 3932160 | tf_op jit(solution)/shard_map/reduce_scatter | solution.py:60
  128.5 11.0 %copy-start.1 = (f32[3072,512]{1,0:T(8,128)S(1)}, f32[3072,512]{1,0:T(8,128)}, u32[]{:S(2)}) copy-start(f32[3072,512]{1,0:T(8,128)} %copy.50) | copy-start | bytes 18874372
  130.9 8.6 %collective-permute-start.2 = (f32[2,4,192,512]{3,2,1,0:T(8,128)S(1)}, f32[2,4,192,512]{3,2,1,0:T(8,128)S(1)}, u32[]{:S(2)}, u32[]{:S(2)}) collective-permute-start(f32[2,4,192,512]{3,2,1,0:T(8,128)S(1)} %dynamic-slice_bitcast_fusion), channel_id=1, source_target_pairs={{0,1},{1,0},{2,3},{3,2},{4,5},{5,4},{6,7},{7,6},{8,9},{9,8},{10,11... | collective-permute-start | bytes 9437192 | tf_op jit(solution)/shard_map/ppermute | solution.py:58
  142.2 109.7 %reduce-scatter.9.cloned.1.call-start = ((), (), s32[]{:S(2)}) async-start(), calls=%async_computation.9 | async-start | bytes 1966080 | tf_op jit(solution)/shard_map/reduce_scatter | solution.py:81
  145.4 59.2 %collective-permute-start.4 = (f32[192,1024]{1,0:T(8,128)S(1)}, f32[192,1024]{1,0:T(8,128)S(1)}, u32[]{:S(2)}, u32[]{:S(2)}) collective-permute-start(f32[192,1024]{1,0:T(8,128)S(1)} %copy.55), channel_id=1, source_target_pairs={{0,0},{16,1},{32,2},{48,3},{64,4},{80,5},{96,6},{112,7},{1,8},{17,... | collective-permute-start | bytes 2359304 | tf_op jit(solution)/shard_map/ppermute | solution.py:71
  151.1 51.6 %collective-permute-start.1 = (f32[192,512]{1,0:T(8,128)S(1)}, f32[192,512]{1,0:T(8,128)}, u32[]{:S(2)}, u32[]{:S(2)}) collective-permute-start(f32[192,512]{1,0:T(8,128)S(1)} %dynamic-slice_bitcast_fusion.3), channel_id=1, source_target_pairs={{0,8},{8,0},{1,9},{9,1},{2,10},{10,2},{3,11},{11,3},{4,12},{12,4},... | collective-permute-start | bytes 1179656 | tf_op jit(solution)/shard_map/ppermute | solution.py:63
  198.1 13.9 %collective-permute-start.3 = (f32[192,512]{1,0:T(8,128)}, f32[192,512]{1,0:T(8,128)S(1)}, u32[]{:S(2)}, u32[]{:S(2)}) collective-permute-start(f32[192,512]{1,0:T(8,128)} %dynamic-slice_bitcast_fusion.2), channel_id=1, source_target_pairs={{0,8},{8,0},{1,9},{9,1},{2,10},{10,2},{3,11},{11,3},{4,12},{12,4},... | collective-permute-start | bytes 1179656 | tf_op jit(solution)/shard_map/ppermute | solution.py:63
  204.6 9.2 %copy-start.5 = (f32[192,1024]{1,0:T(8,128)}, f32[192,1024]{1,0:T(8,128)S(1)}, u32[]{:S(2)}) copy-start(f32[192,1024]{1,0:T(8,128)S(1)} %collective-permute-done.4) | copy-start | bytes 2359300
  212.0 1.8 copy-start.7
  213.8 4.3 %copy-start.3 = (f32[512,512]{1,0:T(8,128)}, f32[512,512]{1,0:T(8,128)S(1)}, u32[]{:S(2)}) copy-start(f32[512,512]{1,0:T(8,128)S(1)} %fusion.10) | copy-start | bytes 3145732
  218.1 4.4 %collective-permute-start.5 = (f32[768,512]{1,0:T(8,128)}, f32[768,512]{1,0:T(8,128)}, u32[]{:S(2)}, u32[]{:S(2)}) collective-permute-start(f32[768,512]{1,0:T(8,128)} %fusion.2), channel_id=1, source_target_pairs={{0,1},{1,0},{2,3},{3,2},{4,5},{5,4},{6,7},{7,6},{8,9},{9,8},{10,11... | collective-permute-start | bytes 4718600 | tf_op jit(solution)/shard_map/ppermute | solution.py:80
  226.0 135.0 %copy-start.6 = (f32[384,512]{1,0:T(8,128)S(1)}, f32[384,512]{1,0:T(8,128)}, u32[]{:S(2)}) copy-start(f32[384,512]{1,0:T(8,128)} %reduce-scatter.7.cloned.1.call-done) | copy-start | bytes 2359300
  226.0 135.0 %copy-start.8 = (f32[192,512]{1,0:T(8,128)S(1)}, f32[192,512]{1,0:T(8,128)}, u32[]{:S(2)}) copy-start(f32[192,512]{1,0:T(8,128)} %copy-done.7) | copy-start | bytes 1179652
  226.0 135.5 %copy-start.9 = (f32[1,192,512]{2,1,0:T(8,128)S(1)}, f32[1,192,512]{2,1,0:T(8,128)}, u32[]{:S(2)}) copy-start(f32[1,192,512]{2,1,0:T(8,128)} %get-tuple-element.30) | copy-start | bytes 1179652
  226.0 47.8 %reduce-scatter.11.cloned.1.call-start = ((), (), s32[]{:S(2)}) async-start(), calls=%async_computation.10 | async-start | bytes 491520 | tf_op jit(solution)/shard_map/reduce_scatter | solution.py:82
  251.9 65.4 %all-reduce.2.cloned.1.call-start = ((), (), s32[]{:S(2)}) async-start(), calls=%async_computation.11 | async-start | bytes 196608 | tf_op jit(solution)/shard_map/psum | solution.py:83
  273.9 86.2 %all-gather.8.cloned.1.call-start = ((), (), s32[]{:S(2)}) async-start(), calls=%async_computation.12 | async-start | bytes 1966080 | tf_op jit(solution)/shard_map/all_gather | solution.py:85
  360.1 28.1 %collective-permute-start.6 = (f32[768,512]{1,0:T(8,128)}, f32[768,512]{1,0:T(8,128)}, u32[]{:S(2)}, u32[]{:S(2)}) collective-permute-start(f32[768,512]{1,0:T(8,128)} %all-gather.8.cloned.1.call-done), channel_id=1, source_target_pairs={{0,1},{1,0},{2,3},{3,2},{4,5},{5,4},{6,7},{7,6},{8,9},{9,8},{10,11... | collective-permute-start | bytes 4718600 | tf_op jit(solution)/shard_map/ppermute | solution.py:86
  362.8 22.6 %all-to-all-start = ((f32[2,192,512]{1,0,2:T(2,128)}), f32[2,192,512]{1,0,2:T(2,128)S(1)}, u32[]{:S(2)}, u32[]{:S(2)}) async-start(f32[2,192,512]{1,0,2:T(2,128)} %copy.52), calls=%async_computation.2 | async-start | bytes 2097152 | tf_op jit(solution)/shard_map/all_to_all | solution.py:101
  391.8 2.2 copy-start.2
  391.8 2.0 copy-start.10
  394.0 2.4 copy-start.4
Sparse Core Ops, SparseCore 0:
  10.2 44.9 all-gather.3
  57.4 43.7 all-gather.5
  103.7 40.2 reduce-scatter.4
  146.2 50.0 reduce-scatter.6
  226.1 25.7 reduce-scatter.8
  254.2 19.6 reduce-scatter.10
  276.1 41.1 all-reduce.1
  330.2 29.8 all-gather.7
where the time goes:
time: 408 us; the launch traced here: 407 us
  waiting for transfers between devices  248 us (61%)
  matrix products  53.1 us (13%)
  local copies, waits for them, and re-layouts  34.9 us (9%)
  starting transfers between devices  23.8 us (6%)
  other arithmetic  19.8 us (5%)
  between operations  14.4 us (4%)
  blocking collectives  12.7 us (3%)
    dot_general x8, matrix products, product(): lax.dot_general(left, right, (contract, ((), ())), precision=lax.Precisio...  53.1 us
    reduce_scatter x2, waiting for transfers between devices, row_sum(): lax.psum_scatter(chip, 'y', scatter_dimension=0, tiled=True)  44.6 us
    psum x1, waiting for transfers between devices, per_device(): piece = lax.psum(piece, ('xl', 'xh'))  43.5 us
    all_gather x1, waiting for transfers between devices, per_device(): lax.all_gather(masked(lhat_one, mask_one), ROW, axis=1, tiled=True)  43.3 us
    all_gather x1, waiting for transfers between devices, per_device(): piece = lax.all_gather(piece, 'y', axis=0, tiled=True)  30 us
    reduce_scatter x1, waiting for transfers between devices, per_device(): piece = lax.psum_scatter(piece, 'y', scatter_dimension=0, tiled=True)  25.9 us
    reduce_scatter x1, waiting for transfers between devices, per_device(): piece = lax.psum_scatter(piece, 'z', scatter_dimension=0, tiled=True)  21.9 us
    all_to_all x1, waiting for transfers between devices, per_device(): out = lax.all_to_all(out, COL, split_axis=2, concat_axis=1, tiled=True)  17.1 us
  transfers between devices with their start and end apart: 16, of which 12 were waited for; matrix products, arithmetic and copies ran while one was open for 20% of the time, Pallas kernels for 0%

commit v1 on v0

--- a/solution.py
+++ b/solution.py
@@ -9,6 +9,12 @@
 ALL = ROW + COL
 SIZES = (2, 4, 2, 4, 2)
 SWAP = ((0, 1), (1, 0))
+
+
+def summed_here(x, mesh_axis):
+    shards = lax.all_gather(x, mesh_axis, axis=0, tiled=False)
+    total = shards.sum(axis=0)
+    return total
 
 
 def product(left, right, contract=((1,), (0,))):
@@ -80,7 +86,7 @@
     piece = keep + lax.ppermute(send, "core", SWAP)
     piece = lax.psum_scatter(piece, "y", scatter_dimension=0, tiled=True)
     piece = lax.psum_scatter(piece, "z", scatter_dimension=0, tiled=True)
-    piece = lax.psum(piece, ("xl", "xh"))
+    piece = summed_here(piece, ("xl", "xh"))
     piece = lax.all_gather(piece, "z", axis=0, tiled=True)
     piece = lax.all_gather(piece, "y", axis=0, tiled=True)
     other = lax.ppermute(piece, "core", SWAP)

time: 408 us -> 385 us (0.944)
  waiting for transfers between devices: 248 us -> 203 us
  local copies, waits for them, and re-layouts: 34.9 us -> 47.1 us
  blocking collectives: 12.7 us -> 22.5 us
    psum x1 -> x0, waiting for transfers between devices: 43.5 us -> none  [per_device(): piece = lax.psum(piece, ('xl', 'xh'))]
    all_gather x0 -> x1, blocking collectives: none -> 11.9 us  [summed_here(): shards = lax.all_gather(x, mesh_axis, axis=0, tiled=False)]
    unnamed x23 -> x20, local copies, waits for them, and re-layouts: 1.36 us -> 8.66 us
    all_to_all x1, waiting for transfers between devices: 17.1 us -> 12.1 us  [per_device(): out = lax.all_to_all(out, COL, split_axis=2, concat_axis=1, tiled=True)]
  transfers between devices with their start and end apart: 16 -> 15, of which waited for: 12 -> 11; matrix products, arithmetic and copies ran while one was open for 20% -> 24% of each run, Pallas kernels for 0% -> 0%
where the time goes in v1:
time: 385 us; the launch traced here: 384 us
  waiting for transfers between devices  203 us (53%)
  matrix products  53.1 us (14%)
  local copies, waits for them, and re-layouts  47.1 us (12%)
  starting transfers between devices  23.9 us (6%)
  blocking collectives  22.5 us (6%)
  other arithmetic  19.6 us (5%)
  between operations  14.4 us (4%)
    dot_general x8, matrix products, product(): lax.dot_general(left, right, (contract, ((), ())), precision=lax.Precisio...  53.1 us
    reduce_scatter x2, waiting for transfers between devices, row_sum(): lax.psum_scatter(chip, 'y', scatter_dimension=0, tiled=True)  44.6 us
    all_gather x1, waiting for transfers between devices, per_device(): lax.all_gather(masked(lhat_one, mask_one), ROW, axis=1, tiled=True)  43.3 us
    all_gather x1, waiting for transfers between devices, per_device(): piece = lax.all_gather(piece, 'y', axis=0, tiled=True)  33.3 us
    reduce_scatter x1, waiting for transfers between devices, per_device(): piece = lax.psum_scatter(piece, 'y', scatter_dimension=0, tiled=True)  25.9 us
    reduce_scatter x1, waiting for transfers between devices, per_device(): piece = lax.psum_scatter(piece, 'z', scatter_dimension=0, tiled=True)  21.8 us
    dot_general x2, local copies, waits for them, and re-layouts, product(): lax.dot_general(left, right, (contract, ((), ())), precision=lax.Precisio...  13.2 us
    all_to_all x1, waiting for transfers between devices, per_device(): out = lax.all_to_all(out, COL, split_axis=2, concat_axis=1, tiled=True)  12.1 us
  transfers between devices with their start and end apart: 15, of which 11 were waited for; matrix products, arithmetic and copies ran while one was open for 24% of the time, Pallas kernels for 0%

profile of v1, /device:TPU:1, one launch (start us, length us, event | category | flops | bytes accessed | tf_op | source)
XLA Modules:
  0.0 383.9 jit_solution(13337004832124991004)
XLA Ops:
  7.2 0.8 dynamic-slice_convert_fusion
  8.2 1.8 broadcast_multiply_fusion.1
  10.1 1.8 broadcast_multiply_fusion
  11.9 43.3 %all-gather.5.cloned.1.call-done = f32[1536,512]{0,1:T(8,128)} async-done(((f32[1536,64]{0,1:T(8,128)}), f32[1536,512]{0,1:T(8,128)}) %all-gather.5.cloned.1.call-update) | async-done | bytes 3145744 | tf_op jit(solution)/shard_map/all_gather | solution.py:71
  55.2 20.6 %convolution_bitcast_fusion.1 = f32[3072,512]{0,1:T(8,128)} fusion(f32[1536,512]{0,1:T(8,128)} %all-gather.5.cloned.1.call-done, f32[3072,1536]{1,0:T(8,128)} %param.8), kind=kOutput, calls=%fused_computation.1 | convolution fusion | flops 14495514624 | bytes 28311552 | tf_op jit(solution)/shard_map/dot_general | solution.py:21
  75.8 6.6 %copy.59 = f32[3072,512]{1,0:T(8,128)} copy(f32[3072,512]{0,1:T(8,128)} %convolution_bitcast_fusion.1) | data formatting | bytes 12582912 | tf_op jit(solution)/shard_map/dot_general | solution.py:21
  82.5 3.9 %dynamic-slice_bitcast_fusion.1 = f32[2,4,192,512]{3,2,1,0:T(8,128)} fusion(f32[2,4,2,192,512]{4,3,2,1,0:T(8,128)} %bitcast.75, s32[]{:T(128)S(6)} %select_n.42), kind=kLoop, calls=%fused_computation.12 | loop fusion | bytes 6291460 | tf_op jit(solution)/shard_map/jit(dynamic_index_in_dim)/squeeze | solution.py:63
  86.4 3.0 collective-permute-start
  89.4 5.6 %collective-permute-done = f32[2,4,192,512]{3,2,1,0:T(8,128)} collective-permute-done((f32[2,4,192,512]{3,2,1,0:T(8,128)}, f32[2,4,192,512]{3,2,1,0:T(8,128)}, u32[]{:S(2)}, u32[]{:S(2)}) %collective-permute-start) | collective-permute-done | bytes 3145760 | tf_op jit(solution)/shard_map/ppermute | solution.py:64
  95.1 3.6 fusion.1
  98.7 2.0 copy.60
  100.8 0.5 all-gather.7.cloned.1.call-done
  101.3 20.6 %convolution_bitcast_fusion = f32[3072,512]{0,1:T(8,128)} fusion(f32[1536,512]{0,1:T(8,128)} %all-gather.7.cloned.1.call-done, f32[3072,1536]{1,0:T(8,128)} %param.8), kind=kOutput, calls=%fused_computation | convolution fusion | flops 14495514624 | bytes 28311552 | tf_op jit(solution)/shard_map/dot_general | solution.py:21
  121.9 6.6 %copy.61 = f32[3072,512]{1,0:T(8,128)} copy(f32[3072,512]{0,1:T(8,128)} %convolution_bitcast_fusion) | data formatting | bytes 12582912 | tf_op jit(solution)/shard_map/dot_general | solution.py:21
  128.5 2.4 dynamic-slice_bitcast_fusion
  130.9 3.3 collective-permute-start.2
  134.2 5.3 %collective-permute-done.2 = f32[2,4,192,512]{3,2,1,0:T(8,128)S(1)} collective-permute-done((f32[2,4,192,512]{3,2,1,0:T(8,128)S(1)}, f32[2,4,192,512]{3,2,1,0:T(8,128)S(1)}, u32[]{:S(2)}, u32[]{:S(2)}) %collective-permute-start.2) | collective-permute-done | bytes 3145760 | tf_op jit(solution)/shard_map/ppermute | solution.py:64
  139.5 0.7 fusion
  140.3 1.9 copy.62
  142.3 1.3 constant_dynamic-slice_fusion
  143.6 1.4 constant_dynamic-slice_fusion.1
  145.0 0.3 copy.66
  145.4 4.6 %collective-permute-start.4 = (f32[192,1024]{1,0:T(8,128)S(1)}, f32[192,1024]{1,0:T(8,128)S(1)}, u32[]{:S(2)}, u32[]{:S(2)}) collective-permute-start(f32[192,1024]{1,0:T(8,128)S(1)} %copy.66), channel_id=1, source_target_pairs={{0,0},{16,1},{32,2},{48,3},{64,4},{80,5},{96,6},{112,7},{1,8},{17,... | collective-permute-start | bytes 2359304 | tf_op jit(solution)/shard_map/ppermute | solution.py:77
  150.0 1.0 dynamic-slice_bitcast_fusion.3
  151.1 0.6 collective-permute-start.1
  151.6 44.6 %reduce-scatter.7.cloned.1.call-done = f32[384,512]{1,0:T(8,128)} async-done(((f32[1536,512]{1,0:T(8,128)}), f32[384,512]{1,0:T(8,128)}) %reduce-scatter.7.cloned.1.call-update) | async-done | bytes 786448 | tf_op jit(solution)/shard_map/reduce_scatter | solution.py:66
  196.3 1.8 dynamic-slice_bitcast_fusion.2
  198.0 4.6 %collective-permute-start.3 = (f32[192,512]{1,0:T(8,128)}, f32[192,512]{1,0:T(8,128)S(1)}, u32[]{:S(2)}, u32[]{:S(2)}) collective-permute-start(f32[192,512]{1,0:T(8,128)} %dynamic-slice_bitcast_fusion.2), channel_id=1, source_target_pairs={{0,8},{8,0},{1,9},{9,1},{2,10},{10,2},{3,11},{11,3},{4,12},{12,4},... | collective-permute-start | bytes 1179656 | tf_op jit(solution)/shard_map/ppermute | solution.py:69
  202.7 1.9 negate_bitcast_fusion
  204.6 7.3 %collective-permute-done.3 = f32[192,512]{1,0:T(8,128)S(1)} collective-permute-done((f32[192,512]{1,0:T(8,128)}, f32[192,512]{1,0:T(8,128)S(1)}, u32[]{:S(2)}, u32[]{:S(2)}) %collective-permute-start.3) | collective-permute-done | bytes 393248 | tf_op jit(solution)/shard_map/ppermute | solution.py:69
  212.0 1.8 fusion.10
  213.8 2.6 fusion.14
  216.4 1.7 fusion.2
  218.1 1.0 collective-permute-start.5
  219.1 3.4 collective-permute-done.5
  222.5 3.4 fusion.4
  226.0 25.9 %reduce-scatter.9.cloned.1.call-done = f32[192,512]{1,0:T(8,128)} async-done(((f32[768,512]{1,0:T(8,128)}), f32[192,512]{1,0:T(8,128)}) %reduce-scatter.9.cloned.1.call-update) | async-done | bytes 393232 | tf_op jit(solution)/shard_map/reduce_scatter | solution.py:87
  252.0 21.8 %reduce-scatter.11.cloned.1.call-done = f32[48,512]{1,0:T(8,128)} async-done(((f32[192,512]{1,0:T(8,128)}), f32[48,512]{1,0:T(8,128)}) %reduce-scatter.11.cloned.1.call-update) | async-done | bytes 98320 | tf_op jit(solution)/shard_map/reduce_scatter | solution.py:88
  273.8 11.9 %all-gather = f32[192,512]{1,0:T(8,128)S(1)} all-gather(f32[48,512]{1,0:T(8,128)} %reduce-scatter.11.cloned.1.call-done), channel_id=2, replica_groups=mesh['xl'=2,'z'=4,'xh'=2,'y'=4,'core'=2] {'xl','xh'}, dimensions={0}, use_global_device_ids=true | all-gather | bytes 491520 | tf_op jit(solution)/shard_map/all_gather | solution.py:15
  285.8 10.6 %all_gather.22 = f32[192,512]{1,0:T(8,128)} all-gather(f32[48,512]{1,0:T(8,128)S(1)} %reduce_sum.9), channel_id=1, replica_groups=mesh['xl'=2,'z'=4,'xh'=2,'y'=4,'core'=2] {'z'}, dimensions={0}, use_global_device_ids=true | all-gather | bytes 491520 | tf_op jit(solution)/shard_map/all_gather | solution.py:90
  296.4 33.3 %all-gather.9.cloned.1.call-done = f32[768,512]{1,0:T(8,128)} async-done(((f32[192,512]{1,0:T(8,128)}), f32[768,512]{1,0:T(8,128)}) %all-gather.9.cloned.1.call-update) | async-done | bytes 1572880 | tf_op jit(solution)/shard_map/all_gather | solution.py:91
  329.6 1.9 copy.68
  331.5 0.9 collective-permute-start.6
  332.4 1.5 fusion.5
  334.0 1.1 pad_maximum_fusion.1
  335.0 1.3 copy.63
  336.3 5.5 %all-to-all-start = ((f32[2,192,512]{1,0,2:T(2,128)}), f32[2,192,512]{1,0,2:T(2,128)}, u32[]{:S(2)}, u32[]{:S(2)}) async-start(f32[2,192,512]{1,0,2:T(2,128)} %copy.63), calls=%async_computation.2 | async-start | bytes 2097152 | tf_op jit(solution)/shard_map/all_to_all | solution.py:107
  341.8 2.5 copy.70
  344.4 2.5 copy.72
  346.9 12.1 %all-to-all-done = f32[2,192,512]{1,0,2:T(2,128)} async-done(((f32[2,192,512]{1,0,2:T(2,128)}), f32[2,192,512]{1,0,2:T(2,128)}, u32[]{:S(2)}, u32[]{:S(2)}) %all-to-all-start) | async-done | bytes 786464 | tf_op jit(solution)/shard_map/all_to_all | solution.py:107
  359.0 1.3 copy.64
  360.3 0.9 fusion.13
  361.2 0.3 copy.65
  361.5 1.0 squeeze.40
  362.5 1.3 copy.71
  363.8 1.0 squeeze.41
  364.8 2.4 maximum_select_fusion
  367.3 1.0 fusion.8
  368.3 1.0 copy-done.4
  369.3 0.2 slice_add_fusion.1
  369.5 2.0 bitcast_subtract_fusion
  371.5 1.3 copy.74
  372.8 2.9 fusion.7
  375.7 1.3 copy.75
  (37 shorter events, 0.7 us)
Async XLA Ops:
  7.2 325.3 %copy-start = (f32[512,512]{1,0:T(8,128)S(1)}, f32[512,512]{1,0:T(8,128)}, u32[]{:S(2)}) copy-start(f32[512,512]{1,0:T(8,128)} %param.11) | copy-start | bytes 3145732
  7.2 48.0 %all-gather.5.cloned.1.call-start = ((), (), s32[]{:S(2)}) async-start(), calls=%async_computation.5 | async-start | bytes 3538944 | tf_op jit(solution)/shard_map/all_gather | solution.py:71
  10.0 91.3 %all-gather.7.cloned.1.call-start = ((), (), s32[]{:S(2)}) async-start(), calls=%async_computation.7 | async-start | bytes 3538944 | tf_op jit(solution)/shard_map/all_gather | solution.py:72
  11.9 138.1 %reduce-scatter.5.cloned.1.call-start = ((), (), s32[]{:S(2)}) async-start(), calls=%async_computation.6 | async-start | bytes 3932160 | tf_op jit(solution)/shard_map/reduce_scatter | solution.py:66
  86.4 8.7 %collective-permute-start = (f32[2,4,192,512]{3,2,1,0:T(8,128)}, f32[2,4,192,512]{3,2,1,0:T(8,128)}, u32[]{:S(2)}, u32[]{:S(2)}) collective-permute-start(f32[2,4,192,512]{3,2,1,0:T(8,128)} %dynamic-slice_bitcast_fusion.1), channel_id=1, source_target_pairs={{0,1},{1,0},{2,3},{3,2},{4,5},{5,4},{6,7},{7,6},{8,9},{9,8},{10,11... | collective-permute-start | bytes 9437192 | tf_op jit(solution)/shard_map/ppermute | solution.py:64
  100.8 95.5 %reduce-scatter.7.cloned.1.call-start = ((), (), s32[]{:S(2)}) async-start(), calls=%async_computation.8 | async-start | bytes 3932160 | tf_op jit(solution)/shard_map/reduce_scatter | solution.py:66
  128.5 11.0 %copy-start.1 = (f32[3072,512]{1,0:T(8,128)S(1)}, f32[3072,512]{1,0:T(8,128)}, u32[]{:S(2)}) copy-start(f32[3072,512]{1,0:T(8,128)} %copy.61) | copy-start | bytes 18874372
  130.9 8.6 %collective-permute-start.2 = (f32[2,4,192,512]{3,2,1,0:T(8,128)S(1)}, f32[2,4,192,512]{3,2,1,0:T(8,128)S(1)}, u32[]{:S(2)}, u32[]{:S(2)}) collective-permute-start(f32[2,4,192,512]{3,2,1,0:T(8,128)S(1)} %dynamic-slice_bitcast_fusion), channel_id=1, source_target_pairs={{0,1},{1,0},{2,3},{3,2},{4,5},{5,4},{6,7},{7,6},{8,9},{9,8},{10,11... | collective-permute-start | bytes 9437192 | tf_op jit(solution)/shard_map/ppermute | solution.py:64
  142.2 109.7 %reduce-scatter.9.cloned.1.call-start = ((), (), s32[]{:S(2)}) async-start(), calls=%async_computation.9 | async-start | bytes 1966080 | tf_op jit(solution)/shard_map/reduce_scatter | solution.py:87
  145.4 59.2 %collective-permute-start.4 = (f32[192,1024]{1,0:T(8,128)S(1)}, f32[192,1024]{1,0:T(8,128)S(1)}, u32[]{:S(2)}, u32[]{:S(2)}) collective-permute-start(f32[192,1024]{1,0:T(8,128)S(1)} %copy.66), channel_id=1, source_target_pairs={{0,0},{16,1},{32,2},{48,3},{64,4},{80,5},{96,6},{112,7},{1,8},{17,... | collective-permute-start | bytes 2359304 | tf_op jit(solution)/shard_map/ppermute | solution.py:77
  151.1 51.6 %collective-permute-start.1 = (f32[192,512]{1,0:T(8,128)S(1)}, f32[192,512]{1,0:T(8,128)}, u32[]{:S(2)}, u32[]{:S(2)}) collective-permute-start(f32[192,512]{1,0:T(8,128)S(1)} %dynamic-slice_bitcast_fusion.3), channel_id=1, source_target_pairs={{0,8},{8,0},{1,9},{9,1},{2,10},{10,2},{3,11},{11,3},{4,12},{12,4},... | collective-permute-start | bytes 1179656 | tf_op jit(solution)/shard_map/ppermute | solution.py:69
  198.0 13.9 %collective-permute-start.3 = (f32[192,512]{1,0:T(8,128)}, f32[192,512]{1,0:T(8,128)S(1)}, u32[]{:S(2)}, u32[]{:S(2)}) collective-permute-start(f32[192,512]{1,0:T(8,128)} %dynamic-slice_bitcast_fusion.2), channel_id=1, source_target_pairs={{0,8},{8,0},{1,9},{9,1},{2,10},{10,2},{3,11},{11,3},{4,12},{12,4},... | collective-permute-start | bytes 1179656 | tf_op jit(solution)/shard_map/ppermute | solution.py:69
  204.6 9.2 %copy-start.5 = (f32[192,1024]{1,0:T(8,128)}, f32[192,1024]{1,0:T(8,128)S(1)}, u32[]{:S(2)}) copy-start(f32[192,1024]{1,0:T(8,128)S(1)} %collective-permute-done.4) | copy-start | bytes 2359300
  212.0 1.8 copy-start.6
  213.8 4.3 %copy-start.3 = (f32[512,512]{1,0:T(8,128)}, f32[512,512]{1,0:T(8,128)S(1)}, u32[]{:S(2)}) copy-start(f32[512,512]{1,0:T(8,128)S(1)} %fusion.10) | copy-start | bytes 3145732
  218.1 4.4 %collective-permute-start.5 = (f32[768,512]{1,0:T(8,128)}, f32[768,512]{1,0:T(8,128)}, u32[]{:S(2)}, u32[]{:S(2)}) collective-permute-start(f32[768,512]{1,0:T(8,128)} %fusion.2), channel_id=1, source_target_pairs={{0,1},{1,0},{2,3},{3,2},{4,5},{5,4},{6,7},{7,6},{8,9},{9,8},{10,11... | collective-permute-start | bytes 4718600 | tf_op jit(solution)/shard_map/ppermute | solution.py:86
  225.9 106.5 %copy-start.7 = (f32[192,512]{1,0:T(8,128)S(1)}, f32[192,512]{1,0:T(8,128)}, u32[]{:S(2)}) copy-start(f32[192,512]{1,0:T(8,128)} %copy-done.6) | copy-start | bytes 1179652
  225.9 47.9 %reduce-scatter.11.cloned.1.call-start = ((), (), s32[]{:S(2)}) async-start(), calls=%async_computation.10 | async-start | bytes 491520 | tf_op jit(solution)/shard_map/reduce_scatter | solution.py:88
  251.9 77.7 %all-gather.9.cloned.1.call-start = ((), (), s32[]{:S(2)}) async-start(), calls=%async_computation.11 | async-start | bytes 1966080 | tf_op jit(solution)/shard_map/all_gather | solution.py:91
  331.5 33.3 %collective-permute-start.6 = (f32[768,512]{0,1:T(8,128)S(1)}, f32[768,512]{0,1:T(8,128)}, u32[]{:S(2)}, u32[]{:S(2)}) collective-permute-start(f32[768,512]{0,1:T(8,128)S(1)} %copy.68), channel_id=1, source_target_pairs={{0,1},{1,0},{2,3},{3,2},{4,5},{5,4},{6,7},{7,6},{8,9},{9,8},{10,11... | collective-permute-start | bytes 4718600 | tf_op jit(solution)/shard_map/ppermute | solution.py:92
  336.3 22.7 %all-to-all-start = ((f32[2,192,512]{1,0,2:T(2,128)}), f32[2,192,512]{1,0,2:T(2,128)}, u32[]{:S(2)}, u32[]{:S(2)}) async-start(f32[2,192,512]{1,0,2:T(2,128)} %copy.63), calls=%async_computation.2 | async-start | bytes 2097152 | tf_op jit(solution)/shard_map/all_to_all | solution.py:107
  367.2 2.2 copy-start.2
  367.3 2.0 copy-start.4
Sparse Core Ops, SparseCore 0:
  10.2 44.9 all-gather.4
  57.4 43.7 all-gather.6
  103.7 40.2 reduce-scatter.4
  146.2 49.9 reduce-scatter.6
  226.1 25.7 reduce-scatter.8
  254.1 19.6 reduce-scatter.10
  296.5 33.1 all-gather.8
